TPU v7x, 32 devices: a whole 2x2x4 slice. The times are simulated.
32 devices in a mesh: phase: 16 (over z, y, x), lat: 2 (over core).
Axes of the slice: x: 2, y: 2, z: 4, core: 2. Of those that a mesh axis runs over, the one named last changes fastest.
Arguments:
- state_now: float32 [3, 64, 1024], P(None, ('lat', 'phase')), may hold values from -4 to 4
- ocean_depth: float32 [64, 1024], P('lat'), may hold values from 0.5 to 1.5
- coriolis: float32 [64], P('lat'), may hold values from -0.4 to 0.4
- phase_times: float32 [16], P('phase'), may hold values from -6 to 6
- phase_weights: float32 [16], P('phase'), may hold values from 0.00625 to 0.25
Outputs:
- state_next: float32 [3, 64, 1024], P(None, ('lat', 'phase'))
- tendency: float32 [3, 64, 1024], P(None, ('lat', 'phase'))
All inputs are finite; a program needn't handle non-finite values.
Results may differ from a plain program's by a relative error of at most 0.00002.
Values sent between devices are 32-bit elements; how exact they have to be, the bound alone decides.
A program may use at most 64 MiB of HBM per device.

v0:
```python
import math
import jax
import jax.numpy as jnp
from jax import lax
from jax.sharding import PartitionSpec as P

DEG = 8
DEPTH = 4
radius_scale = 2.5
time_step = 0.5
series_terms = 20


def extended(shard, sides, width):
    for axis, dim in sides:
        devices, length = (lax.axis_size(axis), shard.shape[dim])
        up = [(i, (i + 1) % devices) for i in range(devices - 1)]
        down = [(j, i) for i, j in up]
        last = lax.slice_in_dim(shard, length - width, length, axis=dim)
        first = lax.slice_in_dim(shard, 0, width, axis=dim)
        before = lax.ppermute(last, axis, up)
        after = lax.ppermute(first, axis, down)
        shard = jnp.concatenate([before, shard, after], axis=dim)
    return shard


def along_lon(values):
    return (jnp.roll(values, -1, axis=-1) - jnp.roll(values, 1, axis=-1)) * 0.5


def along_lat(values):
    return (values[..., 2:, :] - values[..., :-2, :]) * 0.5


def interior(values):
    return values[..., 1:-1, :]


def wave_operator(fields, coefficients):
    height = fields[:, 0]
    eastward = fields[:, 1]
    northward = fields[:, 2]
    depth_field = coefficients[0]
    rotation = coefficients[1]
    out_height = -(along_lon(interior(depth_field * eastward)) + along_lat(depth_field * northward))
    out_east = -along_lon(interior(height)) + interior(rotation * northward)
    out_north = -along_lat(height) - interior(rotation * eastward)
    return jnp.stack([out_height, out_east, out_north], axis=1) / radius_scale


def advection(fields):
    height = fields[:, 0]
    eastward = fields[:, 1]
    northward = fields[:, 2]
    mid_east = interior(eastward)
    mid_north = interior(northward)
    out_height = -(along_lon(interior(height * eastward)) + along_lat(height * northward))
    out_east = -(mid_east * along_lon(mid_east) + mid_north * along_lat(eastward))
    out_north = -(mid_east * along_lon(mid_north) + mid_north * along_lat(northward))
    return jnp.stack([out_height, out_east, out_north], axis=1)


def series_coeffs(sample_time):
    half_time = sample_time * 0.5
    square = half_time * half_time
    result = []
    for degree in range(DEG + 1):
        summed = jnp.zeros_like(sample_time)
        term_sq = jnp.ones_like(sample_time)
        for series in range(series_terms):
            factor = (-1.0) ** series / (math.factorial(series) * math.factorial(series + degree))
            summed = summed + factor * term_sq
            term_sq = term_sq * square
        result.append(summed * half_time**degree)
    return result


def trimmed(values, have, wanted):
    excess = have - wanted
    if excess == 0:
        return values
    return values[:, :, excess : values.shape[2] - excess]


def per_device(state_now, ocean_depth, coriolis, phase_times, phase_weights):
    tile_rows = ocean_depth.shape[0]
    lat_count = lax.axis_size("lat")
    lat_place = lax.axis_index("lat")
    stacked = jnp.stack([ocean_depth, jnp.broadcast_to(coriolis[:, None], ocean_depth.shape)])
    coefficients = extended(stacked, (("lat", 1),), DEPTH)
    global_rows = lat_place * tile_rows - DEPTH + jnp.arange(tile_rows + 2 * DEPTH, dtype=jnp.int32)
    inside = ((global_rows >= 0) & (global_rows < tile_rows * lat_count)).astype(jnp.float32)
    forward = series_coeffs(phase_times)
    backward = series_coeffs(-phase_times)
    sample_count = phase_times.shape[0]

    def band_coeffs(margin):
        return coefficients[:, DEPTH - margin : DEPTH + tile_rows + margin]

    def band_inside(margin):
        return inside[DEPTH - margin : DEPTH + tile_rows + margin][None, None, :, None]

    def exponential(fields, series):
        accumulated = series[0][:, None, None, None] * fields
        previous = None
        current = fields
        width_prev = 0
        width_cur = 0
        for degree in range(1, DEG + 1):
            if (degree - 1) % DEPTH == 0:
                if previous is None:
                    current = extended(current, (("lat", 2),), DEPTH)
                else:
                    joined = jnp.concatenate(
                        [trimmed(previous, width_prev, 0), trimmed(current, width_cur, 0)], axis=0
                    )
                    joined = extended(joined, (("lat", 2),), DEPTH)
                    previous = joined[:sample_count]
                    current = joined[sample_count:]
                    width_prev = DEPTH
                width_cur = DEPTH
            width_new = width_cur - 1
            applied = wave_operator(current, band_coeffs(width_cur))
            if previous is None:
                advanced = applied
            else:
                advanced = 2.0 * applied + trimmed(previous, width_prev, width_new)
            advanced = advanced * band_inside(width_new)
            accumulated = accumulated + 2.0 * series[degree][:, None, None, None] * trimmed(
                advanced, width_new, 0
            )
            previous = current
            width_prev = width_cur
            current = advanced
            width_cur = width_new
        return accumulated

    def averaged(whole_tile):
        samples = whole_tile[None]
        waves = exponential(samples, forward)
        rimmed = extended(waves, (("lat", 2),), 1)
        pulled = advection(rimmed)
        returned = exponential(pulled, backward)
        return jnp.sum(phase_weights[:, None, None, None] * returned, axis=0)

    whole_tile = lax.all_gather(state_now, "phase", axis=1, tiled=True)

    def summed_whole(partial_value):
        return lax.psum(partial_value, "phase")

    first = summed_whole(averaged(whole_tile))
    middle = whole_tile + time_step * first
    second = summed_whole(averaged(middle))
    tendency_tile = 0.5 * (first + second)
    share = state_now.shape[1]
    start = lax.axis_index("phase") * share
    tendency = lax.dynamic_slice_in_dim(tendency_tile, start, share, 1)
    state_next = state_now + time_step * tendency
    return (state_next, tendency)


def solution(mesh):
    placed = (P(None, ("lat", "phase"), None), P("lat", None), P("lat"), P("phase"), P("phase"))
    return jax.shard_map(
        per_device,
        mesh=mesh,
        in_specs=placed,
        out_specs=(P(None, ("lat", "phase"), None), P(None, ("lat", "phase"), None)),
        check_vma=False,
    )
```

profile of v0, /device:TPU:0, one launch (start us, length us, event | category | flops | bytes accessed | tf_op | source)
XLA Modules:
  0.0 368.3 jit_solution(13352655160559666389)
XLA Ops:
  7.2 0.8 copy.168
  8.0 45.3 %all_gather.3 = f32[3,32,1024]{2,0,1:T(4,128)S(1)} all-gather(f32[3,2,1024]{2,0,1:T(4,128)S(1)} %copy.168), channel_id=1, replica_groups=mesh['phase'=16,'lat'=2] {'phase'}, dimensions={1}, use_global_device_ids=true | all-gather | bytes 417792 | tf_op jit(solution)/shard_map/all_gather | solution.py:146
  53.3 0.2 copy.179
  53.6 1.4 collective-permute-start.3
  55.0 3.0 collective-permute-start.2
  58.2 1.3 collective-permute-start.1
  59.5 3.0 collective-permute-start
  62.8 0.5 collective-permute-done
  64.0 0.2 fusion.311
  67.0 1.3 collective-permute-start.5
  68.3 3.0 collective-permute-start.4
  73.0 0.2 pad_maximum_fusion
  73.9 0.1 fusion.271
  74.1 0.1 fusion.16
  74.8 0.1 fusion.261
  75.8 0.7 fusion.49
  76.5 1.3 collective-permute-start.7
  77.8 3.0 collective-permute-start.6
  80.9 0.8 collective-permute-done.6
  82.5 0.2 fusion.451
  82.7 1.3 collective-permute-start.9
  84.0 3.0 collective-permute-start.8
  87.1 0.9 collective-permute-done.8
  88.6 0.1 fusion.251
  89.4 0.1 fusion.241
  91.5 1.3 collective-permute-start.11
  92.8 3.2 collective-permute-start.10
  97.5 0.2 pad_maximum_fusion.1
  98.4 0.1 fusion.211
  98.5 0.1 fusion.11
  100.2 1.3 fusion.41
  101.6 104.9 %all-reduce.3.cloned.1.call-done = f32[3,32,1024]{2,1,0:T(8,128)} async-done(((f32[3,32,1024]{2,1,0:T(8,128)}), f32[3,32,1024]{2,1,0:T(8,128)}) %all-reduce.3.cloned.1.call-update) | async-done | bytes 393232 | tf_op jit(solution)/shard_map/psum | solution.py:149
  206.5 1.2 fusion.500
  207.8 1.3 collective-permute-start.13
  209.1 3.0 collective-permute-start.12
  212.1 0.9 collective-permute-done.12
  214.5 0.1 fusion.181
  215.4 0.1 fusion.171
  215.5 0.1 fusion.8
  216.6 1.3 collective-permute-start.15
  217.9 3.0 collective-permute-start.14
  220.9 0.9 collective-permute-done.14
  222.6 0.2 pad_maximum_fusion.2
  223.5 0.1 fusion.151
  223.6 0.1 fusion.6
  224.4 0.1 fusion.141
  224.5 0.1 fusion.5
  225.4 0.9 copy-done
  226.2 0.7 fusion.31
  227.0 1.3 collective-permute-start.17
  228.3 3.0 collective-permute-start.16
  231.3 0.8 collective-permute-done.16
  232.9 0.2 fusion.397
  233.2 1.3 collective-permute-start.19
  234.5 3.3 collective-permute-start.18
  237.8 0.6 collective-permute-done.18
  241.9 1.3 collective-permute-start.21
  243.2 3.0 collective-permute-start.20
  246.3 0.9 collective-permute-done.20
  247.9 0.2 pad_maximum_fusion.3
  249.0 0.1 fusion.1
  250.7 1.3 fusion.23
  252.0 107.9 %all-reduce.5.cloned.1.call-done = f32[3,32,1024]{2,1,0:T(8,128)} async-done(((f32[3,32,1024]{2,1,0:T(8,128)}), f32[3,32,1024]{2,1,0:T(8,128)}) %all-reduce.5.cloned.1.call-update) | async-done | bytes 393232 | tf_op jit(solution)/shard_map/psum | solution.py:149
  359.9 1.5 multiply_add_fusion.1
  (340 shorter events, 26.2 us)
Async XLA Ops:
  7.2 199.3 %all-reduce.3.cloned.1.call-start = ((), (), s32[]{:S(2)}) async-start(), calls=%async_computation | async-start | bytes 786432 | tf_op jit(solution)/shard_map/psum | solution.py:149
  53.5 4.6 %copy-start.1 = (f32[32,1024]{1,0:T(8,128)S(1)}, f32[32,1024]{1,0:T(8,128)}, u32[]{:S(2)}) copy-start(f32[32,1024]{1,0:T(8,128)} %param.6) | copy-start | bytes 393220
  53.6 4.5 %copy-start.3 = (f32[32]{0:T(128)S(1)}, f32[32]{0:T(128)}, u32[]{:S(2)}) copy-start(f32[32]{0:T(128)} %param.7) | copy-start | bytes 388
  53.6 9.8 %collective-permute-start.3 = (f32[1,3,4,1024]{3,2,1,0:T(4,128)S(1)}, f32[1,3,4,1024]{3,2,1,0:T(4,128)S(1)}, u32[]{:S(2)}, u32[]{:S(2)}) collective-permute-start(f32[1,3,4,1024]{3,2,1,0:T(4,128)S(1)} %get-tuple-element.195), channel_id=1, source_target_pairs={{1,0},{3,2},{5,4},{7,6},{9,8},{11,10},{13,12},{15,14},{17,16},{19,... | collective-permute-start | bytes 147464 | tf_op jit(solution)/shard_map/ppermute | solution.py:22
  55.0 8.4 %collective-permute-start.2 = (f32[1,3,4,1024]{3,2,1,0:T(4,128)S(1)}, f32[1,3,4,1024]{3,2,1,0:T(4,128)S(1)}, u32[]{:S(2)}, u32[]{:S(2)}) collective-permute-start(f32[1,3,4,1024]{3,2,1,0:T(4,128)S(1)} %get-tuple-element.194), channel_id=1, source_target_pairs={{0,1},{2,3},{4,5},{6,7},{8,9},{10,11},{12,13},{14,15},{16,17},{18,... | collective-permute-start | bytes 147464 | tf_op jit(solution)/shard_map/ppermute | solution.py:21
  58.2 4.6 %collective-permute-start.1 = (f32[2,4,1024]{2,1,0:T(4,128)S(1)}, f32[2,4,1024]{2,1,0:T(4,128)S(1)}, u32[]{:S(2)}, u32[]{:S(2)}) collective-permute-start(f32[2,4,1024]{2,1,0:T(4,128)S(1)} %get-tuple-element.205), channel_id=1, source_target_pairs={{1,0},{3,2},{5,4},{7,6},{9,8},{11,10},{13,12},{15,14},{17,16},{19,... | collective-permute-start | bytes 98312 | tf_op jit(solution)/shard_map/ppermute | solution.py:22
  59.5 3.9 %collective-permute-start = (f32[2,4,1024]{2,1,0:T(4,128)S(1)}, f32[2,4,1024]{2,1,0:T(4,128)S(1)}, u32[]{:S(2)}, u32[]{:S(2)}) collective-permute-start(f32[2,4,1024]{2,1,0:T(4,128)S(1)} %get-tuple-element.204), channel_id=1, source_target_pairs={{0,1},{2,3},{4,5},{6,7},{8,9},{10,11},{12,13},{14,15},{16,17},{18,... | collective-permute-start | bytes 98312 | tf_op jit(solution)/shard_map/ppermute | solution.py:21
  67.0 5.3 %collective-permute-start.5 = (f32[2,3,4,1024]{3,2,1,0:T(4,128)S(1)}, f32[2,3,4,1024]{3,2,1,0:T(4,128)S(1)}, u32[]{:S(2)}, u32[]{:S(2)}) collective-permute-start(f32[2,3,4,1024]{3,2,1,0:T(4,128)S(1)} %get-tuple-element.91), channel_id=1, source_target_pairs={{1,0},{3,2},{5,4},{7,6},{9,8},{11,10},{13,12},{15,14},{17,16},{19,... | collective-permute-start | bytes 294920 | tf_op jit(solution)/shard_map/ppermute | solution.py:22
  68.3 4.0 %collective-permute-start.4 = (f32[2,3,4,1024]{3,2,1,0:T(4,128)S(1)}, f32[2,3,4,1024]{3,2,1,0:T(4,128)S(1)}, u32[]{:S(2)}, u32[]{:S(2)}) collective-permute-start(f32[2,3,4,1024]{3,2,1,0:T(4,128)S(1)} %get-tuple-element.90), channel_id=1, source_target_pairs={{0,1},{2,3},{4,5},{6,7},{8,9},{10,11},{12,13},{14,15},{16,17},{18,... | collective-permute-start | bytes 294920 | tf_op jit(solution)/shard_map/ppermute | solution.py:21
  76.5 4.3 %collective-permute-start.7 = (f32[1,3,1,1024]{3,2,1,0:T(1,128)S(1)}, f32[1,3,1,1024]{3,2,1,0:T(1,128)S(1)}, u32[]{:S(2)}, u32[]{:S(2)}) collective-permute-start(f32[1,3,1,1024]{3,2,1,0:T(1,128)S(1)} %get-tuple-element.193), channel_id=1, source_target_pairs={{1,0},{3,2},{5,4},{7,6},{9,8},{11,10},{13,12},{15,14},{17,16},{19,... | collective-permute-start | bytes 36872 | tf_op jit(solution)/shard_map/ppermute | solution.py:22
  77.8 3.9 %collective-permute-start.6 = (f32[1,3,1,1024]{3,2,1,0:T(1,128)S(1)}, f32[1,3,1,1024]{3,2,1,0:T(1,128)S(1)}, u32[]{:S(2)}, u32[]{:S(2)}) collective-permute-start(f32[1,3,1,1024]{3,2,1,0:T(1,128)S(1)} %get-tuple-element.192), channel_id=1, source_target_pairs={{0,1},{2,3},{4,5},{6,7},{8,9},{10,11},{12,13},{14,15},{16,17},{18,... | collective-permute-start | bytes 36872 | tf_op jit(solution)/shard_map/ppermute | solution.py:21
  82.7 4.3 %collective-permute-start.9 = (f32[1,3,4,1024]{3,2,1,0:T(4,128)S(1)}, f32[1,3,4,1024]{3,2,1,0:T(4,128)S(1)}, u32[]{:S(2)}, u32[]{:S(2)}) collective-permute-start(f32[1,3,4,1024]{3,2,1,0:T(4,128)S(1)} %get-tuple-element.191), channel_id=1, source_target_pairs={{1,0},{3,2},{5,4},{7,6},{9,8},{11,10},{13,12},{15,14},{17,16},{19,... | collective-permute-start | bytes 147464 | tf_op jit(solution)/shard_map/ppermute | solution.py:22
  84.0 3.9 %collective-permute-start.8 = (f32[1,3,4,1024]{3,2,1,0:T(4,128)S(1)}, f32[1,3,4,1024]{3,2,1,0:T(4,128)S(1)}, u32[]{:S(2)}, u32[]{:S(2)}) collective-permute-start(f32[1,3,4,1024]{3,2,1,0:T(4,128)S(1)} %get-tuple-element.190), channel_id=1, source_target_pairs={{0,1},{2,3},{4,5},{6,7},{8,9},{10,11},{12,13},{14,15},{16,17},{18,... | collective-permute-start | bytes 147464 | tf_op jit(solution)/shard_map/ppermute | solution.py:21
  91.5 5.2 %collective-permute-start.11 = (f32[2,3,4,1024]{3,2,1,0:T(4,128)S(1)}, f32[2,3,4,1024]{3,2,1,0:T(4,128)S(1)}, u32[]{:S(2)}, u32[]{:S(2)}) collective-permute-start(f32[2,3,4,1024]{3,2,1,0:T(4,128)S(1)} %get-tuple-element.89), channel_id=1, source_target_pairs={{1,0},{3,2},{5,4},{7,6},{9,8},{11,10},{13,12},{15,14},{17,16},{19,... | collective-permute-start | bytes 294920 | tf_op jit(solution)/shard_map/ppermute | solution.py:22
  92.8 4.0 %collective-permute-start.10 = (f32[2,3,4,1024]{3,2,1,0:T(4,128)S(1)}, f32[2,3,4,1024]{3,2,1,0:T(4,128)S(1)}, u32[]{:S(2)}, u32[]{:S(2)}) collective-permute-start(f32[2,3,4,1024]{3,2,1,0:T(4,128)S(1)} %get-tuple-element.88), channel_id=1, source_target_pairs={{0,1},{2,3},{4,5},{6,7},{8,9},{10,11},{12,13},{14,15},{16,17},{18,... | collective-permute-start | bytes 294920 | tf_op jit(solution)/shard_map/ppermute | solution.py:21
  101.6 258.3 %all-reduce.5.cloned.1.call-start = ((), (), s32[]{:S(2)}) async-start(), calls=%async_computation.1 | async-start | bytes 786432 | tf_op jit(solution)/shard_map/psum | solution.py:149
  207.8 4.3 %collective-permute-start.13 = (f32[1,3,4,1024]{3,2,1,0:T(4,128)S(1)}, f32[1,3,4,1024]{3,2,1,0:T(4,128)S(1)}, u32[]{:S(2)}, u32[]{:S(2)}) collective-permute-start(f32[1,3,4,1024]{3,2,1,0:T(4,128)S(1)} %get-tuple-element.189), channel_id=1, source_target_pairs={{1,0},{3,2},{5,4},{7,6},{9,8},{11,10},{13,12},{15,14},{17,16},{19,... | collective-permute-start | bytes 147464 | tf_op jit(solution)/shard_map/ppermute | solution.py:22
  209.1 3.9 %collective-permute-start.12 = (f32[1,3,4,1024]{3,2,1,0:T(4,128)S(1)}, f32[1,3,4,1024]{3,2,1,0:T(4,128)S(1)}, u32[]{:S(2)}, u32[]{:S(2)}) collective-permute-start(f32[1,3,4,1024]{3,2,1,0:T(4,128)S(1)} %get-tuple-element.188), channel_id=1, source_target_pairs={{0,1},{2,3},{4,5},{6,7},{8,9},{10,11},{12,13},{14,15},{16,17},{18,... | collective-permute-start | bytes 147464 | tf_op jit(solution)/shard_map/ppermute | solution.py:21
  216.6 4.3 %collective-permute-start.15 = (f32[2,3,4,1024]{3,2,1,0:T(4,128)S(1)}, f32[2,3,4,1024]{3,2,1,0:T(4,128)S(1)}, u32[]{:S(2)}, u32[]{:S(2)}) collective-permute-start(f32[2,3,4,1024]{3,2,1,0:T(4,128)S(1)} %get-tuple-element.87), channel_id=1, source_target_pairs={{1,0},{3,2},{5,4},{7,6},{9,8},{11,10},{13,12},{15,14},{17,16},{19,... | collective-permute-start | bytes 294920 | tf_op jit(solution)/shard_map/ppermute | solution.py:22
  217.9 4.0 %collective-permute-start.14 = (f32[2,3,4,1024]{3,2,1,0:T(4,128)S(1)}, f32[2,3,4,1024]{3,2,1,0:T(4,128)S(1)}, u32[]{:S(2)}, u32[]{:S(2)}) collective-permute-start(f32[2,3,4,1024]{3,2,1,0:T(4,128)S(1)} %get-tuple-element.86), channel_id=1, source_target_pairs={{0,1},{2,3},{4,5},{6,7},{8,9},{10,11},{12,13},{14,15},{16,17},{18,... | collective-permute-start | bytes 294920 | tf_op jit(solution)/shard_map/ppermute | solution.py:21
  225.2 1.0 copy-start
  227.0 4.3 %collective-permute-start.17 = (f32[1,3,1,1024]{3,2,1,0:T(1,128)S(1)}, f32[1,3,1,1024]{3,2,1,0:T(1,128)S(1)}, u32[]{:S(2)}, u32[]{:S(2)}) collective-permute-start(f32[1,3,1,1024]{3,2,1,0:T(1,128)S(1)} %get-tuple-element.187), channel_id=1, source_target_pairs={{1,0},{3,2},{5,4},{7,6},{9,8},{11,10},{13,12},{15,14},{17,16},{19,... | collective-permute-start | bytes 36872 | tf_op jit(solution)/shard_map/ppermute | solution.py:22
  228.3 3.9 %collective-permute-start.16 = (f32[1,3,1,1024]{3,2,1,0:T(1,128)S(1)}, f32[1,3,1,1024]{3,2,1,0:T(1,128)S(1)}, u32[]{:S(2)}, u32[]{:S(2)}) collective-permute-start(f32[1,3,1,1024]{3,2,1,0:T(1,128)S(1)} %get-tuple-element.186), channel_id=1, source_target_pairs={{0,1},{2,3},{4,5},{6,7},{8,9},{10,11},{12,13},{14,15},{16,17},{18,... | collective-permute-start | bytes 36872 | tf_op jit(solution)/shard_map/ppermute | solution.py:21
  233.2 4.6 %collective-permute-start.19 = (f32[1,3,4,1024]{3,2,1,0:T(4,128)S(1)}, f32[1,3,4,1024]{3,2,1,0:T(4,128)S(1)}, u32[]{:S(2)}, u32[]{:S(2)}) collective-permute-start(f32[1,3,4,1024]{3,2,1,0:T(4,128)S(1)} %get-tuple-element.185), channel_id=1, source_target_pairs={{1,0},{3,2},{5,4},{7,6},{9,8},{11,10},{13,12},{15,14},{17,16},{19,... | collective-permute-start | bytes 147464 | tf_op jit(solution)/shard_map/ppermute | solution.py:22
  234.5 3.9 %collective-permute-start.18 = (f32[1,3,4,1024]{3,2,1,0:T(4,128)S(1)}, f32[1,3,4,1024]{3,2,1,0:T(4,128)S(1)}, u32[]{:S(2)}, u32[]{:S(2)}) collective-permute-start(f32[1,3,4,1024]{3,2,1,0:T(4,128)S(1)} %get-tuple-element.184), channel_id=1, source_target_pairs={{0,1},{2,3},{4,5},{6,7},{8,9},{10,11},{12,13},{14,15},{16,17},{18,... | collective-permute-start | bytes 147464 | tf_op jit(solution)/shard_map/ppermute | solution.py:21
  241.9 4.3 %collective-permute-start.21 = (f32[2,3,4,1024]{3,2,1,0:T(4,128)S(1)}, f32[2,3,4,1024]{3,2,1,0:T(4,128)S(1)}, u32[]{:S(2)}, u32[]{:S(2)}) collective-permute-start(f32[2,3,4,1024]{3,2,1,0:T(4,128)S(1)} %get-tuple-element.85), channel_id=1, source_target_pairs={{1,0},{3,2},{5,4},{7,6},{9,8},{11,10},{13,12},{15,14},{17,16},{19,... | collective-permute-start | bytes 294920 | tf_op jit(solution)/shard_map/ppermute | solution.py:22
  243.2 4.0 %collective-permute-start.20 = (f32[2,3,4,1024]{3,2,1,0:T(4,128)S(1)}, f32[2,3,4,1024]{3,2,1,0:T(4,128)S(1)}, u32[]{:S(2)}, u32[]{:S(2)}) collective-permute-start(f32[2,3,4,1024]{3,2,1,0:T(4,128)S(1)} %get-tuple-element.84), channel_id=1, source_target_pairs={{0,1},{2,3},{4,5},{6,7},{8,9},{10,11},{12,13},{14,15},{16,17},{18,... | collective-permute-start | bytes 294920 | tf_op jit(solution)/shard_map/ppermute | solution.py:21
  252.0 107.9 %copy-start.2 = (f32[3,2,1024]{2,1,0:T(2,128)S(1)}, f32[3,2,1024]{2,1,0:T(2,128)}, u32[]{:S(2)}) copy-start(f32[3,2,1024]{2,1,0:T(2,128)} %param.5) | copy-start | bytes 73732
Sparse Core Ops, SparseCore 0:
  101.7 104.7 all-reduce.2
  252.1 107.7 all-reduce.4
where the time goes:
time: 369 us; the launch traced here: 368 us
  waiting for transfers between devices  219 us (59%)
  starting transfers between devices  48.2 us (13%)
  blocking collectives  45.3 us (12%)
  other arithmetic  21.8 us (6%)
  between operations  17.7 us (5%)
  local copies, waits for them, and re-layouts  16.1 us (4%)
    psum x2, waiting for transfers between devices, summed_whole(): return lax.psum(partial_value, 'phase')  213 us
    all_gather x1, blocking collectives, per_device(): whole_tile = lax.all_gather(state_now, 'phase', axis=1, tiled=True)  45.3 us
    ppermute x11, starting transfers between devices, extended(): before = lax.ppermute(last, axis, up)  33.8 us
    ppermute x11, starting transfers between devices, extended(): after = lax.ppermute(first, axis, down)  14.3 us
    slice x140, local copies, waits for them, and re-layouts, along_lon(): return (jnp.roll(values, -1, axis=-1) - jnp.roll(values, 1, axis=-1)) * 0.5  12.7 us
    another operation x63, other arithmetic, wave_operator(): return jnp.stack([out_height, out_east, out_north], axis=1) / radius_scale  7.91 us
  transfers between devices with their start and end apart: 24, of which 10 were waited for; matrix products, arithmetic and copies ran while one was open for 0% of the time, Pallas kernels for 0%

commit v1 on v0

--- a/solution.py
+++ b/solution.py
@@ -9,6 +9,27 @@
 radius_scale = 2.5
 time_step = 0.5
 series_terms = 20
+
+
+def handle_the_roots(xin, pos_dim=1):
+    ax_name = "phase"
+    kept_rows = [xin]
+    to_i = 0
+    n_chips = lax.axis_size(ax_name)
+    while to_i < n_chips - 1:
+        kept_rows.append(
+            lax.ppermute(
+                kept_rows[-1],
+                axis_name=ax_name,
+                perm=[(s, (s + 1) % n_chips) for s in range(n_chips)],
+            )
+        )
+        to_i = to_i + 1
+    return jnp.roll(
+        jnp.concatenate(kept_rows[::-1], axis=pos_dim),
+        shift=(lax.axis_index(ax_name) + 1) * xin.shape[pos_dim],
+        axis=pos_dim,
+    )
 
 
 def extended(shard, sides, width):
@@ -143,7 +164,7 @@
         returned = exponential(pulled, backward)
         return jnp.sum(phase_weights[:, None, None, None] * returned, axis=0)
 
-    whole_tile = lax.all_gather(state_now, "phase", axis=1, tiled=True)
+    whole_tile = handle_the_roots(state_now)
 
     def summed_whole(partial_value):
         return lax.psum(partial_value, "phase")

time: 369 us -> 431 us (1.17)
  waiting for transfers between devices: 219 us -> 324 us
  blocking collectives: 45.3 us -> 0 us
    ppermute x0 -> x15, waiting for transfers between devices: none -> 105 us  [handle_the_roots(): lax.ppermute(kept_rows[-1], axis_name=ax_name, perm=[(s, (s + 1) % n_chip...]
    all_gather x1 -> x0, blocking collectives: 45.3 us -> none  [per_device(): whole_tile = lax.all_gather(state_now, 'phase', axis=1, tiled=True)]
  transfers between devices with their start and end apart: 24 -> 39, of which waited for: 10 -> 26; matrix products, arithmetic and copies ran while one was open for 0% -> 0% of each run, Pallas kernels for 0% -> 0%
where the time goes in v1:
time: 431 us
  waiting for transfers between devices  324 us (75%)
  starting transfers between devices  51.1 us (12%)
  other arithmetic  21.2 us (5%)
  between operations  17.7 us (4%)
  local copies, waits for them, and re-layouts  16.5 us (4%)
    psum x2, waiting for transfers between devices, summed_whole(): return lax.psum(partial_value, 'phase')  213 us
    ppermute x15, waiting for transfers between devices, handle_the_roots(): lax.ppermute(kept_rows[-1], axis_name=ax_name, perm=[(s, (s + 1) % n_chip...  105 us
    ppermute x11, starting transfers between devices, extended(): before = lax.ppermute(last, axis, up)  33.8 us
    ppermute x11, starting transfers between devices, extended(): after = lax.ppermute(first, axis, down)  14.2 us
    slice x140, local copies, waits for them, and re-layouts, along_lon(): return (jnp.roll(values, -1, axis=-1) - jnp.roll(values, 1, axis=-1)) * 0.5  12.7 us
  transfers between devices with their start and end apart: 39, of which 26 were waited for; matrix products, arithmetic and copies ran while one was open for 0% of the time, Pallas kernels for 0%

profile of v1, /device:TPU:0, one launch (start us, length us, event | category | flops | bytes accessed | tf_op | source)
XLA Modules:
  0.0 430.5 jit_solution(4660687579214937369)
XLA Ops:
  7.2 3.0 collective-permute-start
  10.2 6.0 %collective-permute-done = f32[3,2,1024]{2,1,0:T(2,128)S(1)} collective-permute-done((f32[3,2,1024]{2,1,0:T(2,128)}, f32[3,2,1024]{2,1,0:T(2,128)S(1)}, u32[]{:S(2)}, u32[]{:S(2)}) %collective-permute-start) | collective-permute-done | bytes 24608 | tf_op jit(solution)/shard_map/ppermute | solution.py:21
  16.3 7.4 %collective-permute-done.1 = f32[3,2,1024]{2,1,0:T(2,128)S(1)} collective-permute-done((f32[3,2,1024]{2,1,0:T(2,128)S(1)}, f32[3,2,1024]{2,1,0:T(2,128)S(1)}, u32[]{:S(2)}, u32[]{:S(2)}) %collective-permute-start.1) | collective-permute-done | bytes 24608 | tf_op jit(solution)/shard_map/ppermute | solution.py:21
  23.7 7.4 %collective-permute-done.2 = f32[3,2,1024]{2,1,0:T(2,128)S(1)} collective-permute-done((f32[3,2,1024]{2,1,0:T(2,128)S(1)}, f32[3,2,1024]{2,1,0:T(2,128)S(1)}, u32[]{:S(2)}, u32[]{:S(2)}) %collective-permute-start.2) | collective-permute-done | bytes 24608 | tf_op jit(solution)/shard_map/ppermute | solution.py:21
  31.1 7.4 %collective-permute-done.3 = f32[3,2,1024]{2,1,0:T(2,128)S(1)} collective-permute-done((f32[3,2,1024]{2,1,0:T(2,128)S(1)}, f32[3,2,1024]{2,1,0:T(2,128)S(1)}, u32[]{:S(2)}, u32[]{:S(2)}) %collective-permute-start.3) | collective-permute-done | bytes 24608 | tf_op jit(solution)/shard_map/ppermute | solution.py:21
  38.5 7.4 %collective-permute-done.4 = f32[3,2,1024]{2,1,0:T(2,128)S(1)} collective-permute-done((f32[3,2,1024]{2,1,0:T(2,128)S(1)}, f32[3,2,1024]{2,1,0:T(2,128)S(1)}, u32[]{:S(2)}, u32[]{:S(2)}) %collective-permute-start.4) | collective-permute-done | bytes 24608 | tf_op jit(solution)/shard_map/ppermute | solution.py:21
  45.9 7.4 %collective-permute-done.5 = f32[3,2,1024]{2,1,0:T(2,128)S(1)} collective-permute-done((f32[3,2,1024]{2,1,0:T(2,128)S(1)}, f32[3,2,1024]{2,1,0:T(2,128)S(1)}, u32[]{:S(2)}, u32[]{:S(2)}) %collective-permute-start.5) | collective-permute-done | bytes 24608 | tf_op jit(solution)/shard_map/ppermute | solution.py:21
  53.4 7.4 %collective-permute-done.6 = f32[3,2,1024]{2,1,0:T(2,128)S(1)} collective-permute-done((f32[3,2,1024]{2,1,0:T(2,128)S(1)}, f32[3,2,1024]{2,1,0:T(2,128)S(1)}, u32[]{:S(2)}, u32[]{:S(2)}) %collective-permute-start.6) | collective-permute-done | bytes 24608 | tf_op jit(solution)/shard_map/ppermute | solution.py:21
  60.8 7.4 %collective-permute-done.7 = f32[3,2,1024]{2,1,0:T(2,128)S(1)} collective-permute-done((f32[3,2,1024]{2,1,0:T(2,128)S(1)}, f32[3,2,1024]{2,1,0:T(2,128)S(1)}, u32[]{:S(2)}, u32[]{:S(2)}) %collective-permute-start.7) | collective-permute-done | bytes 24608 | tf_op jit(solution)/shard_map/ppermute | solution.py:21
  68.2 7.4 %collective-permute-done.8 = f32[3,2,1024]{2,1,0:T(2,128)S(1)} collective-permute-done((f32[3,2,1024]{2,1,0:T(2,128)S(1)}, f32[3,2,1024]{2,1,0:T(2,128)S(1)}, u32[]{:S(2)}, u32[]{:S(2)}) %collective-permute-start.8) | collective-permute-done | bytes 24608 | tf_op jit(solution)/shard_map/ppermute | solution.py:21
  75.6 7.4 %collective-permute-done.9 = f32[3,2,1024]{2,1,0:T(2,128)S(1)} collective-permute-done((f32[3,2,1024]{2,1,0:T(2,128)S(1)}, f32[3,2,1024]{2,1,0:T(2,128)S(1)}, u32[]{:S(2)}, u32[]{:S(2)}) %collective-permute-start.9) | collective-permute-done | bytes 24608 | tf_op jit(solution)/shard_map/ppermute | solution.py:21
  83.1 7.5 %collective-permute-done.10 = f32[3,2,1024]{2,1,0:T(2,128)S(1)} collective-permute-done((f32[3,2,1024]{2,1,0:T(2,128)S(1)}, f32[3,2,1024]{2,1,0:T(2,128)S(1)}, u32[]{:S(2)}, u32[]{:S(2)}) %collective-permute-start.10) | collective-permute-done | bytes 24608 | tf_op jit(solution)/shard_map/ppermute | solution.py:21
  90.6 7.4 %collective-permute-done.11 = f32[3,2,1024]{2,1,0:T(2,128)S(1)} collective-permute-done((f32[3,2,1024]{2,1,0:T(2,128)S(1)}, f32[3,2,1024]{2,1,0:T(2,128)S(1)}, u32[]{:S(2)}, u32[]{:S(2)}) %collective-permute-start.11) | collective-permute-done | bytes 24608 | tf_op jit(solution)/shard_map/ppermute | solution.py:21
  98.0 0.7 stack_broadcast_in_dim.2
  98.7 1.3 collective-permute-start.16
  100.0 3.0 collective-permute-start.15
  103.1 2.3 collective-permute-done.12
  105.4 7.4 %collective-permute-done.13 = f32[3,2,1024]{2,1,0:T(2,128)S(1)} collective-permute-done((f32[3,2,1024]{2,1,0:T(2,128)S(1)}, f32[3,2,1024]{2,1,0:T(2,128)S(1)}, u32[]{:S(2)}, u32[]{:S(2)}) %collective-permute-start.13) | collective-permute-done | bytes 24608 | tf_op jit(solution)/shard_map/ppermute | solution.py:21
  113.1 7.1 %collective-permute-done.14 = f32[3,2,1024]{2,1,0:T(2,128)S(1)} collective-permute-done((f32[3,2,1024]{2,1,0:T(2,128)S(1)}, f32[3,2,1024]{2,1,0:T(2,128)S(1)}, u32[]{:S(2)}, u32[]{:S(2)}) %collective-permute-start.14) | collective-permute-done | bytes 24608 | tf_op jit(solution)/shard_map/ppermute | solution.py:21
  120.2 0.7 concatenate.1871
  121.0 1.3 collective-permute-start.18
  122.3 3.0 collective-permute-start.17
  125.4 0.8 collective-permute-done.17
  126.7 0.2 fusion.311
  129.7 1.3 collective-permute-start.20
  131.0 3.0 collective-permute-start.19
  135.8 0.2 pad_maximum_fusion
  138.5 0.6 fusion.49
  139.1 1.3 collective-permute-start.22
  140.4 3.0 collective-permute-start.21
  143.5 0.8 collective-permute-done.21
  145.1 0.2 fusion.451
  145.3 1.3 collective-permute-start.24
  146.6 3.2 collective-permute-start.23
  149.8 0.7 collective-permute-done.23
  154.1 1.3 collective-permute-start.26
  155.3 3.0 collective-permute-start.25
  159.1 0.2 collective-permute-done.25
  160.1 0.2 pad_maximum_fusion.1
  162.8 1.3 fusion.41
  164.2 104.9 %all-reduce.3.cloned.1.call-done = f32[3,32,1024]{2,1,0:T(8,128)} async-done(((f32[3,32,1024]{2,1,0:T(8,128)}), f32[3,32,1024]{2,1,0:T(8,128)}) %all-reduce.3.cloned.1.call-update) | async-done | bytes 393232 | tf_op jit(solution)/shard_map/psum | solution.py:170
  269.1 1.1 fusion.500
  270.2 1.3 collective-permute-start.28
  271.5 3.0 collective-permute-start.27
  274.6 0.9 collective-permute-done.27
  279.0 1.3 collective-permute-start.30
  280.3 3.0 collective-permute-start.29
  283.3 0.9 collective-permute-done.29
  285.0 0.2 pad_maximum_fusion.2
  287.8 0.9 copy-done
  288.6 0.6 fusion.31
  289.2 1.3 collective-permute-start.32
  290.5 3.2 collective-permute-start.31
  293.8 0.6 collective-permute-done.31
  295.2 0.2 fusion.397
  295.4 1.3 collective-permute-start.34
  296.7 3.0 collective-permute-start.33
  299.8 0.9 collective-permute-done.33
  304.2 1.3 collective-permute-start.36
  305.5 3.0 collective-permute-start.35
  308.5 0.9 collective-permute-done.35
  312.9 1.3 fusion.23
  314.3 107.9 %all-reduce.5.cloned.1.call-done = f32[3,32,1024]{2,1,0:T(8,128)} async-done(((f32[3,32,1024]{2,1,0:T(8,128)}), f32[3,32,1024]{2,1,0:T(8,128)}) %all-reduce.5.cloned.1.call-update) | async-done | bytes 393232 | tf_op jit(solution)/shard_map/psum | solution.py:170
  422.1 1.5 multiply_add_fusion.1
  (367 shorter events, 28.3 us)
Async XLA Ops:
  7.2 91.5 %copy-start.1 = (f32[32,1024]{1,0:T(8,128)S(1)}, f32[32,1024]{1,0:T(8,128)}, u32[]{:S(2)}) copy-start(f32[32,1024]{1,0:T(8,128)} %param.6) | copy-start | bytes 393220
  7.2 261.9 %all-reduce.3.cloned.1.call-start = ((), (), s32[]{:S(2)}) async-start(), calls=%async_computation | async-start | bytes 786432 | tf_op jit(solution)/shard_map/psum | solution.py:170
  7.2 9.0 %collective-permute-start = (f32[3,2,1024]{2,1,0:T(2,128)}, f32[3,2,1024]{2,1,0:T(2,128)S(1)}, u32[]{:S(2)}, u32[]{:S(2)}) collective-permute-start(f32[3,2,1024]{2,1,0:T(2,128)} %param.5), channel_id=1, source_target_pairs={{0,2},{2,4},{4,6},{6,8},{8,10},{10,12},{12,14},{14,16},{16,18},{18... | collective-permute-start | bytes 73736 | tf_op jit(solution)/shard_map/ppermute | solution.py:21
  16.3 7.4 %collective-permute-start.1 = (f32[3,2,1024]{2,1,0:T(2,128)S(1)}, f32[3,2,1024]{2,1,0:T(2,128)S(1)}, u32[]{:S(2)}, u32[]{:S(2)}) collective-permute-start(f32[3,2,1024]{2,1,0:T(2,128)S(1)} %collective-permute-done), channel_id=1, source_target_pairs={{0,2},{2,4},{4,6},{6,8},{8,10},{10,12},{12,14},{14,16},{16,18},{18... | collective-permute-start | bytes 73736 | tf_op jit(solution)/shard_map/ppermute | solution.py:21
  23.7 7.4 %collective-permute-start.2 = (f32[3,2,1024]{2,1,0:T(2,128)S(1)}, f32[3,2,1024]{2,1,0:T(2,128)S(1)}, u32[]{:S(2)}, u32[]{:S(2)}) collective-permute-start(f32[3,2,1024]{2,1,0:T(2,128)S(1)} %collective-permute-done.1), channel_id=1, source_target_pairs={{0,2},{2,4},{4,6},{6,8},{8,10},{10,12},{12,14},{14,16},{16,18},{18... | collective-permute-start | bytes 73736 | tf_op jit(solution)/shard_map/ppermute | solution.py:21
  31.1 7.4 %collective-permute-start.3 = (f32[3,2,1024]{2,1,0:T(2,128)S(1)}, f32[3,2,1024]{2,1,0:T(2,128)S(1)}, u32[]{:S(2)}, u32[]{:S(2)}) collective-permute-start(f32[3,2,1024]{2,1,0:T(2,128)S(1)} %collective-permute-done.2), channel_id=1, source_target_pairs={{0,2},{2,4},{4,6},{6,8},{8,10},{10,12},{12,14},{14,16},{16,18},{18... | collective-permute-start | bytes 73736 | tf_op jit(solution)/shard_map/ppermute | solution.py:21
  38.5 7.4 %collective-permute-start.4 = (f32[3,2,1024]{2,1,0:T(2,128)S(1)}, f32[3,2,1024]{2,1,0:T(2,128)S(1)}, u32[]{:S(2)}, u32[]{:S(2)}) collective-permute-start(f32[3,2,1024]{2,1,0:T(2,128)S(1)} %collective-permute-done.3), channel_id=1, source_target_pairs={{0,2},{2,4},{4,6},{6,8},{8,10},{10,12},{12,14},{14,16},{16,18},{18... | collective-permute-start | bytes 73736 | tf_op jit(solution)/shard_map/ppermute | solution.py:21
  45.9 7.4 %collective-permute-start.5 = (f32[3,2,1024]{2,1,0:T(2,128)S(1)}, f32[3,2,1024]{2,1,0:T(2,128)S(1)}, u32[]{:S(2)}, u32[]{:S(2)}) collective-permute-start(f32[3,2,1024]{2,1,0:T(2,128)S(1)} %collective-permute-done.4), channel_id=1, source_target_pairs={{0,2},{2,4},{4,6},{6,8},{8,10},{10,12},{12,14},{14,16},{16,18},{18... | collective-permute-start | bytes 73736 | tf_op jit(solution)/shard_map/ppermute | solution.py:21
  53.4 7.4 %collective-permute-start.6 = (f32[3,2,1024]{2,1,0:T(2,128)S(1)}, f32[3,2,1024]{2,1,0:T(2,128)S(1)}, u32[]{:S(2)}, u32[]{:S(2)}) collective-permute-start(f32[3,2,1024]{2,1,0:T(2,128)S(1)} %collective-permute-done.5), channel_id=1, source_target_pairs={{0,2},{2,4},{4,6},{6,8},{8,10},{10,12},{12,14},{14,16},{16,18},{18... | collective-permute-start | bytes 73736 | tf_op jit(solution)/shard_map/ppermute | solution.py:21
  60.8 7.4 %collective-permute-start.7 = (f32[3,2,1024]{2,1,0:T(2,128)S(1)}, f32[3,2,1024]{2,1,0:T(2,128)S(1)}, u32[]{:S(2)}, u32[]{:S(2)}) collective-permute-start(f32[3,2,1024]{2,1,0:T(2,128)S(1)} %collective-permute-done.6), channel_id=1, source_target_pairs={{0,2},{2,4},{4,6},{6,8},{8,10},{10,12},{12,14},{14,16},{16,18},{18... | collective-permute-start | bytes 73736 | tf_op jit(solution)/shard_map/ppermute | solution.py:21
  68.2 7.4 %collective-permute-start.8 = (f32[3,2,1024]{2,1,0:T(2,128)S(1)}, f32[3,2,1024]{2,1,0:T(2,128)S(1)}, u32[]{:S(2)}, u32[]{:S(2)}) collective-permute-start(f32[3,2,1024]{2,1,0:T(2,128)S(1)} %collective-permute-done.7), channel_id=1, source_target_pairs={{0,2},{2,4},{4,6},{6,8},{8,10},{10,12},{12,14},{14,16},{16,18},{18... | collective-permute-start | bytes 73736 | tf_op jit(solution)/shard_map/ppermute | solution.py:21
  75.6 7.4 %collective-permute-start.9 = (f32[3,2,1024]{2,1,0:T(2,128)S(1)}, f32[3,2,1024]{2,1,0:T(2,128)S(1)}, u32[]{:S(2)}, u32[]{:S(2)}) collective-permute-start(f32[3,2,1024]{2,1,0:T(2,128)S(1)} %collective-permute-done.8), channel_id=1, source_target_pairs={{0,2},{2,4},{4,6},{6,8},{8,10},{10,12},{12,14},{14,16},{16,18},{18... | collective-permute-start | bytes 73736 | tf_op jit(solution)/shard_map/ppermute | solution.py:21
  83.1 7.5 %collective-permute-start.10 = (f32[3,2,1024]{2,1,0:T(2,128)S(1)}, f32[3,2,1024]{2,1,0:T(2,128)S(1)}, u32[]{:S(2)}, u32[]{:S(2)}) collective-permute-start(f32[3,2,1024]{2,1,0:T(2,128)S(1)} %collective-permute-done.9), channel_id=1, source_target_pairs={{0,2},{2,4},{4,6},{6,8},{8,10},{10,12},{12,14},{14,16},{16,18},{18... | collective-permute-start | bytes 73736 | tf_op jit(solution)/shard_map/ppermute | solution.py:21
  90.5 7.4 %collective-permute-start.11 = (f32[3,2,1024]{2,1,0:T(2,128)S(1)}, f32[3,2,1024]{2,1,0:T(2,128)S(1)}, u32[]{:S(2)}, u32[]{:S(2)}) collective-permute-start(f32[3,2,1024]{2,1,0:T(2,128)S(1)} %collective-permute-done.10), channel_id=1, source_target_pairs={{0,2},{2,4},{4,6},{6,8},{8,10},{10,12},{12,14},{14,16},{16,18},{18... | collective-permute-start | bytes 73736 | tf_op jit(solution)/shard_map/ppermute | solution.py:21
  98.0 7.4 %collective-permute-start.12 = (f32[3,2,1024]{2,1,0:T(2,128)S(1)}, f32[3,2,1024]{2,1,0:T(2,128)S(1)}, u32[]{:S(2)}, u32[]{:S(2)}) collective-permute-start(f32[3,2,1024]{2,1,0:T(2,128)S(1)} %collective-permute-done.11), channel_id=1, source_target_pairs={{0,2},{2,4},{4,6},{6,8},{8,10},{10,12},{12,14},{14,16},{16,18},{18... | collective-permute-start | bytes 73736 | tf_op jit(solution)/shard_map/ppermute | solution.py:21
  98.7 26.6 %collective-permute-start.16 = (f32[2,4,1024]{2,1,0:T(4,128)S(1)}, f32[2,4,1024]{2,1,0:T(4,128)S(1)}, u32[]{:S(2)}, u32[]{:S(2)}) collective-permute-start(f32[2,4,1024]{2,1,0:T(4,128)S(1)} %get-tuple-element.205), channel_id=1, source_target_pairs={{1,0},{3,2},{5,4},{7,6},{9,8},{11,10},{13,12},{15,14},{17,16},{19,... | collective-permute-start | bytes 98312 | tf_op jit(solution)/shard_map/ppermute | solution.py:43
  100.0 25.3 %collective-permute-start.15 = (f32[2,4,1024]{2,1,0:T(4,128)S(1)}, f32[2,4,1024]{2,1,0:T(4,128)S(1)}, u32[]{:S(2)}, u32[]{:S(2)}) collective-permute-start(f32[2,4,1024]{2,1,0:T(4,128)S(1)} %get-tuple-element.204), channel_id=1, source_target_pairs={{0,1},{2,3},{4,5},{6,7},{8,9},{10,11},{12,13},{14,15},{16,17},{18,... | collective-permute-start | bytes 98312 | tf_op jit(solution)/shard_map/ppermute | solution.py:42
  103.1 17.2 %copy-start.2 = (f32[3,2,1024]{2,1,0:T(2,128)S(1)}, f32[3,2,1024]{2,1,0:T(2,128)}, u32[]{:S(2)}) copy-start(f32[3,2,1024]{2,1,0:T(2,128)} %param.5) | copy-start | bytes 73732
  105.4 7.4 %collective-permute-start.13 = (f32[3,2,1024]{2,1,0:T(2,128)S(1)}, f32[3,2,1024]{2,1,0:T(2,128)S(1)}, u32[]{:S(2)}, u32[]{:S(2)}) collective-permute-start(f32[3,2,1024]{2,1,0:T(2,128)S(1)} %collective-permute-done.12), channel_id=1, source_target_pairs={{0,2},{2,4},{4,6},{6,8},{8,10},{10,12},{12,14},{14,16},{16,18},{18... | collective-permute-start | bytes 73736 | tf_op jit(solution)/shard_map/ppermute | solution.py:21
  112.8 7.4 %collective-permute-start.14 = (f32[3,2,1024]{2,1,0:T(2,128)S(1)}, f32[3,2,1024]{2,1,0:T(2,128)S(1)}, u32[]{:S(2)}, u32[]{:S(2)}) collective-permute-start(f32[3,2,1024]{2,1,0:T(2,128)S(1)} %collective-permute-done.13), channel_id=1, source_target_pairs={{0,2},{2,4},{4,6},{6,8},{8,10},{10,12},{12,14},{14,16},{16,18},{18... | collective-permute-start | bytes 73736 | tf_op jit(solution)/shard_map/ppermute | solution.py:21
  121.0 4.4 %collective-permute-start.18 = (f32[1,3,4,1024]{3,2,1,0:T(4,128)S(1)}, f32[1,3,4,1024]{3,2,1,0:T(4,128)S(1)}, u32[]{:S(2)}, u32[]{:S(2)}) collective-permute-start(f32[1,3,4,1024]{3,2,1,0:T(4,128)S(1)} %get-tuple-element.195), channel_id=1, source_target_pairs={{1,0},{3,2},{5,4},{7,6},{9,8},{11,10},{13,12},{15,14},{17,16},{19,... | collective-permute-start | bytes 147464 | tf_op jit(solution)/shard_map/ppermute | solution.py:43
  122.3 3.9 collective-permute-start.17
  129.7 5.3 %collective-permute-start.20 = (f32[2,3,4,1024]{3,2,1,0:T(4,128)S(1)}, f32[2,3,4,1024]{3,2,1,0:T(4,128)S(1)}, u32[]{:S(2)}, u32[]{:S(2)}) collective-permute-start(f32[2,3,4,1024]{3,2,1,0:T(4,128)S(1)} %get-tuple-element.91), channel_id=1, source_target_pairs={{1,0},{3,2},{5,4},{7,6},{9,8},{11,10},{13,12},{15,14},{17,16},{19,... | collective-permute-start | bytes 294920 | tf_op jit(solution)/shard_map/ppermute | solution.py:43
  131.0 4.0 collective-permute-start.19
  139.1 4.3 %collective-permute-start.22 = (f32[1,3,1,1024]{3,2,1,0:T(1,128)S(1)}, f32[1,3,1,1024]{3,2,1,0:T(1,128)S(1)}, u32[]{:S(2)}, u32[]{:S(2)}) collective-permute-start(f32[1,3,1,1024]{3,2,1,0:T(1,128)S(1)} %get-tuple-element.193), channel_id=1, source_target_pairs={{1,0},{3,2},{5,4},{7,6},{9,8},{11,10},{13,12},{15,14},{17,16},{19,... | collective-permute-start | bytes 36872 | tf_op jit(solution)/shard_map/ppermute | solution.py:43
  140.4 3.9 collective-permute-start.21
  145.3 4.5 %collective-permute-start.24 = (f32[1,3,4,1024]{3,2,1,0:T(4,128)S(1)}, f32[1,3,4,1024]{3,2,1,0:T(4,128)S(1)}, u32[]{:S(2)}, u32[]{:S(2)}) collective-permute-start(f32[1,3,4,1024]{3,2,1,0:T(4,128)S(1)} %get-tuple-element.191), channel_id=1, source_target_pairs={{1,0},{3,2},{5,4},{7,6},{9,8},{11,10},{13,12},{15,14},{17,16},{19,... | collective-permute-start | bytes 147464 | tf_op jit(solution)/shard_map/ppermute | solution.py:43
  146.6 3.9 collective-permute-start.23
  154.1 5.0 %collective-permute-start.26 = (f32[2,3,4,1024]{3,2,1,0:T(4,128)S(1)}, f32[2,3,4,1024]{3,2,1,0:T(4,128)S(1)}, u32[]{:S(2)}, u32[]{:S(2)}) collective-permute-start(f32[2,3,4,1024]{3,2,1,0:T(4,128)S(1)} %get-tuple-element.89), channel_id=1, source_target_pairs={{1,0},{3,2},{5,4},{7,6},{9,8},{11,10},{13,12},{15,14},{17,16},{19,... | collective-permute-start | bytes 294920 | tf_op jit(solution)/shard_map/ppermute | solution.py:43
  155.3 4.0 collective-permute-start.25
  164.1 258.0 %all-reduce.5.cloned.1.call-start = ((), (), s32[]{:S(2)}) async-start(), calls=%async_computation.1 | async-start | bytes 786432 | tf_op jit(solution)/shard_map/psum | solution.py:170
  270.2 4.3 %collective-permute-start.28 = (f32[1,3,4,1024]{3,2,1,0:T(4,128)S(1)}, f32[1,3,4,1024]{3,2,1,0:T(4,128)S(1)}, u32[]{:S(2)}, u32[]{:S(2)}) collective-permute-start(f32[1,3,4,1024]{3,2,1,0:T(4,128)S(1)} %get-tuple-element.189), channel_id=1, source_target_pairs={{1,0},{3,2},{5,4},{7,6},{9,8},{11,10},{13,12},{15,14},{17,16},{19,... | collective-permute-start | bytes 147464 | tf_op jit(solution)/shard_map/ppermute | solution.py:43
  271.5 3.9 collective-permute-start.27
  279.0 4.3 %collective-permute-start.30 = (f32[2,3,4,1024]{3,2,1,0:T(4,128)S(1)}, f32[2,3,4,1024]{3,2,1,0:T(4,128)S(1)}, u32[]{:S(2)}, u32[]{:S(2)}) collective-permute-start(f32[2,3,4,1024]{3,2,1,0:T(4,128)S(1)} %get-tuple-element.87), channel_id=1, source_target_pairs={{1,0},{3,2},{5,4},{7,6},{9,8},{11,10},{13,12},{15,14},{17,16},{19,... | collective-permute-start | bytes 294920 | tf_op jit(solution)/shard_map/ppermute | solution.py:43
  280.3 4.0 collective-permute-start.29
  287.6 1.0 copy-start
  289.2 4.6 %collective-permute-start.32 = (f32[1,3,1,1024]{3,2,1,0:T(1,128)S(1)}, f32[1,3,1,1024]{3,2,1,0:T(1,128)S(1)}, u32[]{:S(2)}, u32[]{:S(2)}) collective-permute-start(f32[1,3,1,1024]{3,2,1,0:T(1,128)S(1)} %get-tuple-element.187), channel_id=1, source_target_pairs={{1,0},{3,2},{5,4},{7,6},{9,8},{11,10},{13,12},{15,14},{17,16},{19,... | collective-permute-start | bytes 36872 | tf_op jit(solution)/shard_map/ppermute | solution.py:43
  290.5 3.9 collective-permute-start.31
  295.4 4.3 %collective-permute-start.34 = (f32[1,3,4,1024]{3,2,1,0:T(4,128)S(1)}, f32[1,3,4,1024]{3,2,1,0:T(4,128)S(1)}, u32[]{:S(2)}, u32[]{:S(2)}) collective-permute-start(f32[1,3,4,1024]{3,2,1,0:T(4,128)S(1)} %get-tuple-element.185), channel_id=1, source_target_pairs={{1,0},{3,2},{5,4},{7,6},{9,8},{11,10},{13,12},{15,14},{17,16},{19,... | collective-permute-start | bytes 147464 | tf_op jit(solution)/shard_map/ppermute | solution.py:43
  296.7 3.9 collective-permute-start.33
  304.2 4.3 %collective-permute-start.36 = (f32[2,3,4,1024]{3,2,1,0:T(4,128)S(1)}, f32[2,3,4,1024]{3,2,1,0:T(4,128)S(1)}, u32[]{:S(2)}, u32[]{:S(2)}) collective-permute-start(f32[2,3,4,1024]{3,2,1,0:T(4,128)S(1)} %get-tuple-element.85), channel_id=1, source_target_pairs={{1,0},{3,2},{5,4},{7,6},{9,8},{11,10},{13,12},{15,14},{17,16},{19,... | collective-permute-start | bytes 294920 | tf_op jit(solution)/shard_map/ppermute | solution.py:43
  305.5 4.0 collective-permute-start.35
Sparse Core Ops, SparseCore 0:
  164.2 104.7 all-reduce.2
  314.4 107.6 all-reduce.4
